TPU v7x, 768 devices: a whole 4x8x12 slice. The times are simulated.
768 devices in a mesh: occ: 32 (over x_hi, y, core), virt: 24 (over x_lo, z).
Axes of the slice: x: 4 (x_hi: 2, x_lo: 2; x = x_hi * 2 + x_lo), y: 8, z: 12, core: 2. Of those that a mesh axis runs over, the one named last changes fastest.
Arguments:
- amplitudes: bfloat16 [16384, 6144], P('occ'), may hold values from -6 to 6
- amp_map: int32 [256, 48], P('occ'), may hold values 0 or 1
- integrals: bfloat16 [6144, 6144], P('occ', 'virt'), may hold values from -0.078125 to 0.078125
- int_map: int32 [48, 48], P(None, 'virt'), may hold values 0 or 1
- exchange: bfloat16 [16384, 6144], P('occ', 'virt'), may hold values from -0.078125 to 0.078125
- residual_in: float32 [16384, 6144], P('occ', 'virt'), may hold values from -6 to 6
Outputs:
- residual: float32 [16384, 6144], P('occ', 'virt')
- pair_energy: float32 [16384], P('occ')
All inputs are finite; a program needn't handle non-finite values. No bound on the sum of `amp_map` or of `int_map` on one device may be relied on, other than what follows from the above.
Results may differ from a plain program's by a relative error of at most 0.0003.
Values may be sent and summed in bfloat16 or wider, within the bound.
No kernel may reach another device: no remote copies, remote signals or barrier semaphores. Data moves between devices by JAX's collectives and lax.ppermute only.
A program may use at most 32 MiB of HBM per device.

v0:
```python
import jax
import jax.numpy as jnp
from jax import lax
from jax.sharding import PartitionSpec as P

PTILE = 64
VTILE = 128


def on_device(amplitudes, amp_map, integrals, int_map, exchange, residual_in):
    row_tiles = amp_map.shape[0]
    col_tiles = amp_map.shape[1]
    shaped = amplitudes.reshape(row_tiles, PTILE, col_tiles, VTILE)
    amp_masked = (shaped * amp_map.astype(jnp.bfloat16)[:, None, :, None]).reshape(amplitudes.shape)
    full_mask = jnp.repeat(jnp.repeat(int_map, VTILE, axis=0), VTILE, axis=1).astype(jnp.bfloat16)
    panel = lax.all_gather(integrals, "occ", axis=0, tiled=True)
    product = jnp.dot(amp_masked, panel * full_mask, preferred_element_type=jnp.float32)
    residual = residual_in + product
    energy_terms = jnp.sum(residual * exchange.astype(jnp.float32), axis=1)
    pair_energy = lax.psum(energy_terms, "virt")
    return (residual, pair_energy)


def solution(mesh):
    in_specs = (
        P("occ", None),
        P("occ", None),
        P("occ", "virt"),
        P(None, "virt"),
        P("occ", "virt"),
        P("occ", "virt"),
    )
    out_specs = (P("occ", "virt"), P("occ"))
    return jax.shard_map(
        on_device, mesh=mesh, in_specs=in_specs, out_specs=out_specs, check_vma=False
    )
```

profile of v0, /device:TPU:2, one launch (start us, length us, event | category | flops | bytes accessed | tf_op | source)
XLA Modules:
  0.0 186.5 jit_solution(13145264077453916819)
XLA Ops:
  7.2 0.0 all-gather.2.cloned.1.call-start
  7.2 0.7 all-gather.2.cloned.1.call-update
  7.9 0.7 convert_element_type.18
  8.6 0.7 convert_element_type.17
  9.3 0.1 copy.8
  9.4 1.1 copy.10
  10.5 1.2 copy.9
  11.7 99.9 %all-gather.2.cloned.1.call-done = bf16[6144,256]{1,0:T(8,128)(2,1)} async-done(((bf16[192,256]{1,0:T(8,128)(2,1)}), bf16[6144,256]{1,0:T(8,128)(2,1)}) %all-gather.2.cloned.1.call-update) | async-done | bytes 3145744 | tf_op jit(solution)/shard_map/all_gather | solution.py:16
  111.7 0.2 broadcast_in_dim.7
  111.9 7.8 %broadcast_in_dim.8 = bf16[6144,2,128]{2,1,0:T(2,128)(2,1)S(1)} broadcast(bf16[6144,2]{1,0:T(8,128)(2,1)S(1)} %bitcast.19), dimensions={0,1} | broadcast | bytes 3170304 | tf_op jit(solution)/shard_map/broadcast_in_dim | solution.py:15
  119.6 0.0 copy-start
  119.6 0.9 mul.17
  120.5 1.0 copy-done
  121.5 5.7 %multiply_reduce_fusion = (f32[512]{0:T(512)S(1)}, f32[512,256]{0,1:T(8,128)S(1)}) fusion(bf16[512,256]{0,1:T(8,128)(2,1)S(1)} %copy.10, f32[512,256]{0,1:T(8,128)S(1)} %copy.9, bf16[6144,256]{1,0:T(8,128)(2,1)S(1)} %copy-done, bf16[768,8,2,128]{3,2,1,0:T(2,128)(2,1)S(1)} %bitcast.20, bf16[512,6144]{1,0:T(8,128)(2,1)} %param.6, ...), kind=kOutput, calls=%fused_computation.6 | convolution fusion | flops 1615855104 | bytes 20187136 | tf_op jit(solution)/shard_map/dot_general | solution.py:17
  127.2 51.4 %psum.7 = f32[512]{0:T(512)} all-reduce(f32[512]{0:T(512)S(1)} %get-tuple-element.4), channel_id=1, replica_groups=mesh['occ'=32,'virt'=24] {'virt'}, use_global_device_ids=true, to_apply=%region_1.0 | all-reduce | flops 512 | bytes 4096 | tf_op jit(solution)/shard_map/psum | solution.py:20
  178.6 1.0 copy.11
Async XLA Ops:
  7.2 104.5 %all-gather.2.cloned.1.call-start = ((), (), s32[]{:S(2)}) async-start(), calls=%async_computation | async-start | bytes 3244032 | tf_op jit(solution)/shard_map/all_gather | solution.py:16
  119.6 1.9 %copy-start = (bf16[6144,256]{1,0:T(8,128)(2,1)S(1)}, bf16[6144,256]{1,0:T(8,128)(2,1)}, u32[]{:S(2)}) copy-start(bf16[6144,256]{1,0:T(8,128)(2,1)} %all-gather.2.cloned.1.call-done) | copy-start | bytes 9437188
Sparse Core Ops, SparseCore 0:
  11.9 99.6 all-gather.1
where the time goes:
time: 187 us; the launch traced here: 186 us
  waiting for transfers between devices  101 us (54%)
  blocking collectives  51.4 us (27%)
  between operations  14.1 us (8%)
  local copies, waits for them, and re-layouts  13.3 us (7%)
  matrix products  5.68 us (3%)
    all_gather x1, waiting for transfers between devices, on_device(): panel = lax.all_gather(integrals, 'occ', axis=0, tiled=True)  99.9 us
    psum x1, blocking collectives, on_device(): pair_energy = lax.psum(energy_terms, 'virt')  51.4 us
    broadcast_in_dim x1, local copies, waits for them, and re-layouts, on_device(): jnp.repeat(jnp.repeat(int_map, VTILE, axis=0), VTILE, axis=1)  7.75 us
    dot_general x1, matrix products, on_device(): jnp.dot(amp_masked, panel * full_mask, preferred_element_type=jnp.float32)  5.68 us
    unnamed x5, local copies, waits for them, and re-layouts  4.32 us
  transfers between devices with their start and end apart: 1, of which 1 were waited for; matrix products, arithmetic and copies ran while one was open for 2% of the time, Pallas kernels for 0%

commit v1 on v0

v1 whole, which is shorter than its diff:
```python
import jax
import jax.numpy as jnp
from jax import lax
from jax.sharding import Mesh, PartitionSpec as P

PTILE = 64
VTILE = 128
SCALE = 2.0**19


def on_device(amplitudes, amp_map, integrals, int_map, exchange, residual_in):
    row_tiles, col_tiles = amp_map.shape
    rows, columns = residual_in.shape
    shaped = amplitudes.reshape(row_tiles, PTILE, col_tiles, VTILE)
    amp_masked = (shaped * amp_map.astype(jnp.bfloat16)[:, None, :, None]).reshape(amplitudes.shape)

    mine = (integrals.astype(jnp.float32) * SCALE).astype(jnp.float16)
    pair = lax.all_gather(mine, "xh", axis=0, tiled=False)
    panel = lax.all_gather(pair, ("y", "c"), axis=0, tiled=False)
    panel = panel.swapaxes(0, 1).reshape(-1, columns).astype(jnp.bfloat16)
    full_mask = jnp.repeat(jnp.repeat(int_map, VTILE, axis=0), VTILE, axis=1).astype(jnp.bfloat16)

    product = jnp.dot(amp_masked, panel * full_mask, preferred_element_type=jnp.float32)
    residual = residual_in + product * (1.0 / SCALE)
    terms = jnp.sum(residual * exchange.astype(jnp.float32), axis=1)
    ways = lax.axis_size(("xl", "z"))
    terms = lax.all_to_all(jnp.broadcast_to(terms, (ways, rows)), ("xl", "z"), 0, 0, tiled=True)
    return residual, jnp.sum(terms, axis=0)


def solution(mesh):
    fine = Mesh(mesh.devices.reshape(2, 8, 2, 2, 12), ("xh", "y", "c", "xl", "z"))
    occ, virt = ("xh", "y", "c"), ("xl", "z")
    in_specs = (P(occ, None), P(occ, None), P(occ, virt), P(None, virt), P(occ, virt), P(occ, virt))
    return jax.shard_map(on_device, mesh=fine, in_specs=in_specs, out_specs=(P(occ, virt), P(occ)), check_vma=False)
```

time: 187 us -> 85.5 us (0.46)
  the two profiles are of different devices: /device:TPU:2 before, /device:TPU:1 now
where the time goes in v1:
time: 85.5 us; the launch traced here: 85.2 us
  blocking collectives  44.2 us (52%)
  local copies, waits for them, and re-layouts  13.2 us (15%)
  starting transfers between devices  8.94 us (10%)
  waiting for transfers between devices  8.64 us (10%)
  matrix products  5.71 us (7%)
  other arithmetic  3.72 us (4%)
    all_gather x1, blocking collectives, on_device(): panel = lax.all_gather(pair, ('y', 'c'), axis=0, tiled=False)  38 us
    all_to_all x1, starting transfers between devices, on_device(): lax.all_to_all(jnp.broadcast_to(terms, (ways, rows)), ('xl', 'z'), 0, 0,...  8.94 us
    all_to_all x1, waiting for transfers between devices, on_device(): lax.all_to_all(jnp.broadcast_to(terms, (ways, rows)), ('xl', 'z'), 0, 0,...  8.64 us
    broadcast_in_dim x1, local copies, waits for them, and re-layouts, on_device(): jnp.repeat(jnp.repeat(int_map, VTILE, axis=0), VTILE, axis=1)  7.75 us
    all_gather x1, blocking collectives, on_device(): pair = lax.all_gather(mine, 'xh', axis=0, tiled=False)  6.23 us
    dot_general x1, matrix products, on_device(): jnp.dot(amp_masked, panel * full_mask, preferred_element_type=jnp.float32)  5.71 us
    unnamed x3, local copies, waits for them, and re-layouts  3.32 us
  transfers between devices with their start and end apart: 1, of which 1 were waited for; matrix products, arithmetic and copies ran while one was open for 1% of the time, Pallas kernels for 0%

profile of v1, /device:TPU:1, one launch (start us, length us, event | category | flops | bytes accessed | tf_op | source)
XLA Modules:
  0.0 85.2 jit_solution(4749244331578728534)
XLA Ops:
  0.6 0.7 convert_element_type.38
  1.3 0.7 convert_element_type.32
  2.0 0.1 copy.32
  2.1 0.9 %multiply_convert_fusion = f16[192,256]{1,0:T(8,128)(2,1)S(1)} fusion(bf16[192,256]{1,0:T(8,128)(2,1)} %param.8), kind=kLoop, calls=%fused_computation.8 | loop fusion | flops 147456 | bytes 196608 | tf_op jit(solution)/shard_map/convert_element_type | solution.py:17
  3.0 6.2 %all-gather = f16[384,256]{1,0:T(8,128)(2,1)S(1)} all-gather(f16[192,256]{1,0:T(8,128)(2,1)S(1)} %multiply_convert_fusion), channel_id=2, replica_groups=mesh['xh'=2,'y'=8,'c'=2,'xl'=2,'z'=12] {'xh'}, dimensions={0}, use_global_device_ids=true | all-gather | bytes 294912 | tf_op jit(solution)/shard_map/all_gather | solution.py:18
  9.3 1.1 %copy.34 = bf16[512,256]{0,1:T(8,128)(2,1)S(1)} copy(bf16[512,256]{1,0:T(8,128)(2,1)} %param.10) | data formatting | bytes 524288 | tf_op args[4]
  10.4 1.2 %copy.33 = f32[512,256]{0,1:T(8,128)S(1)} copy(f32[512,256]{1,0:T(8,128)} %param.11) | data formatting | bytes 1048576 | tf_op args[5]
  11.6 38.0 %all-gather.3 = f16[32,192,256]{2,1,0:T(8,128)(2,1)S(1)} all-gather(f16[2,192,256]{2,1,0:T(8,128)(2,1)S(1)} %bitcast.32), channel_id=3, replica_groups=mesh['xh'=2,'y'=8,'c'=2,'xl'=2,'z'=12] {'y','c'}, dimensions={0}, use_global_device_ids=true | all-gather | bytes 3342336 | tf_op jit(solution)/shard_map/all_gather | solution.py:19
  49.6 0.8 convert_element_type.42
  50.4 0.3 copy.31
  50.7 0.2 broadcast_in_dim.10
  51.0 7.8 %broadcast_in_dim.11 = bf16[6144,2,128]{2,1,0:T(2,128)(2,1)S(1)} broadcast(bf16[6144,2]{1,0:T(8,128)(2,1)S(1)} %bitcast.29), dimensions={0,1} | broadcast | bytes 3170304 | tf_op jit(solution)/shard_map/broadcast_in_dim | solution.py:21
  58.7 0.9 %mul.29 = bf16[8,64,48,128]{3,2,1,0:T(8,128)(2,1)S(1)} broadcast(bf16[8,48]{1,0:T(8,128)(2,1)S(1)} %convert_element_type.32), dimensions={0,2} | broadcast | bytes 6292224 | tf_op jit(solution)/shard_map/mul | solution.py:15
  59.6 5.7 %multiply_reduce_fusion = (f32[512]{0:T(512)S(1)}, f32[512,256]{0,1:T(8,128)S(1)}) fusion(bf16[512,256]{0,1:T(8,128)(2,1)S(1)} %copy.34, f32[512,256]{0,1:T(8,128)S(1)} %copy.33, bf16[6144,256]{1,0:T(8,128)(2,1)S(1)} %bitcast.30, bf16[768,8,2,128]{3,2,1,0:T(2,128)(2,1)S(1)} %bitcast.31, bf16[512,6144]{1,0:T(8,128)(2,1)} %param.6, ...), kind=kOutput, calls=%fused_computation.7 | convolution fusion | flops 1615986176 | bytes 20187136 | tf_op jit(solution)/shard_map/dot_general | solution.py:23
  65.3 0.6 broadcast_in_dim.12
  66.0 8.9 %all-to-all-start = ((f32[24,1,512]{2,1,0:T(1,128)}), f32[24,1,512]{2,1,0:T(1,128)S(1)}, u32[]{:S(2)}, u32[]{:S(2)}) async-start(f32[24,1,512]{2,1,0:T(1,128)} %broadcast_in_dim.12), calls=%async_computation | async-start | bytes 98304 | tf_op jit(solution)/shard_map/all_to_all | solution.py:27
  74.9 1.0 %copy.36 = f32[512,256]{1,0:T(8,128)} copy(f32[512,256]{0,1:T(8,128)S(1)} %get-tuple-element.15) | data formatting | bytes 1048576
  75.9 8.6 %all-to-all-done = f32[24,1,512]{2,1,0:T(1,128)S(1)} async-done(((f32[24,1,512]{2,1,0:T(1,128)}), f32[24,1,512]{2,1,0:T(1,128)S(1)}, u32[]{:S(2)}, u32[]{:S(2)}) %all-to-all-start) | async-done | bytes 49184 | tf_op jit(solution)/shard_map/all_to_all | solution.py:27
  84.5 0.6 reduce_sum.19
Async XLA Ops:
  66.0 18.6 %all-to-all-start = ((f32[24,1,512]{2,1,0:T(1,128)}), f32[24,1,512]{2,1,0:T(1,128)S(1)}, u32[]{:S(2)}, u32[]{:S(2)}) async-start(f32[24,1,512]{2,1,0:T(1,128)} %broadcast_in_dim.12), calls=%async_computation | async-start | bytes 98304 | tf_op jit(solution)/shard_map/all_to_all | solution.py:27

commit v2 on v1

v2 whole, which is shorter than its diff:
```python
import functools

import jax
import jax.numpy as jnp
from jax import lax
from jax.experimental import pallas as pl
from jax.experimental.pallas import tpu as pltpu
from jax.sharding import Mesh, PartitionSpec as P

PTILE = 64
VTILE = 128
SCALE = 2.0**19


def ladder(shape, amp_map, int_map, amplitudes, panel, exchange, residual_in, residual, terms):
    xh, y, c, part = shape
    rows, columns = residual.shape
    step = 2 * c * part
    chunks = [(h, y0) for h in range(xh) for y0 in range(0, y, 2)]

    total = jnp.zeros((rows, columns), jnp.float32)
    for h, y0 in chunks:
        first = (h * y + y0) * c * part
        right = []
        for at in range(0, step, PTILE):
            block, inner = divmod(at, part)
            source = ((y0 + block // c) * c + block % c) * xh + h
            tiles = []
            for j in range(columns // VTILE):
                keep = int_map[j, (first + at) // VTILE].astype(jnp.bfloat16)
                tiles.append(panel[source, inner : inner + PTILE, j * VTILE : (j + 1) * VTILE] * keep)
            right.append(jnp.concatenate(tiles, axis=1))
        right = jnp.concatenate(right, axis=0)
        left = []
        for r in range(rows // PTILE):
            tiles = []
            for k in range(step // VTILE):
                keep = amp_map[r, first // VTILE + k].astype(jnp.bfloat16)
                tiles.append(amplitudes[r * PTILE : (r + 1) * PTILE, first + k * VTILE : first + (k + 1) * VTILE] * keep)
            left.append(jnp.concatenate(tiles, axis=1))
        left = jnp.concatenate(left, axis=0)
        total += jnp.dot(left, right, preferred_element_type=jnp.float32)
    total = residual_in[...] + total * (1.0 / SCALE)
    residual[...] = total
    product = total * exchange[...].astype(jnp.float32)
    folded = product[:, :VTILE]
    for j in range(1, columns // VTILE):
        folded += product[:, j * VTILE : (j + 1) * VTILE]
    line = jnp.sum(folded.T, axis=0, keepdims=True)
    for i in range(terms.shape[0]):
        terms[i] = line


def on_device(amplitudes, amp_map, integrals, int_map, exchange, residual_in):
    rows, columns = residual_in.shape
    part, depth = integrals.shape[0], amplitudes.shape[1]
    xh, y, c = (lax.axis_size(name) for name in ("xh", "y", "c"))
    ways = lax.axis_size(("xl", "z"))
    mine = (integrals.astype(jnp.float32) * SCALE).astype(jnp.float16)
    pair = lax.all_gather(mine, "xh", axis=0, tiled=False)
    panel = lax.all_gather(pair, ("y", "c"), axis=0, tiled=False)
    panel = panel.reshape(y * c * xh, part, columns).astype(jnp.bfloat16)
    vmem, smem = pl.BlockSpec(memory_space=pltpu.VMEM), pl.BlockSpec(memory_space=pltpu.SMEM)
    residual, terms = pl.pallas_call(
        functools.partial(ladder, (xh, y, c, part)),
        out_shape=(
            jax.ShapeDtypeStruct((rows, columns), jnp.float32),
            jax.ShapeDtypeStruct((ways, 1, rows), jnp.float32),
        ),
        in_specs=[smem, smem, vmem, vmem, vmem, vmem],
        out_specs=(vmem, vmem),
        cost_estimate=pl.CostEstimate(
            flops=2 * rows * depth * columns, bytes_accessed=2 * rows * depth, transcendentals=0
        ),
        compiler_params=pltpu.CompilerParams(vmem_limit_bytes=24 << 20),
        name="ladder",
    )(amp_map, int_map.T, amplitudes, panel, exchange, residual_in)
    terms = lax.all_to_all(terms, ("xl", "z"), 0, 0, tiled=True)
    return residual, jnp.sum(terms, axis=(0, 1))


def solution(mesh):
    fine = Mesh(mesh.devices.reshape(2, 8, 2, 2, 12), ("xh", "y", "c", "xl", "z"))
    occ, virt = ("xh", "y", "c"), ("xl", "z")
    in_specs = (P(occ, None), P(occ, None), P(occ, virt), P(None, virt), P(occ, virt), P(occ, virt))
    return jax.shard_map(on_device, mesh=fine, in_specs=in_specs, out_specs=(P(occ, virt), P(occ)), check_vma=False)
```

time: 85.5 us -> 71.1 us (0.83)
  blocking collectives: 44.2 us -> 62.7 us
  local copies, waits for them, and re-layouts: 13.2 us -> 2.03 us
  starting transfers between devices: 8.94 us -> 0 us
  waiting for transfers between devices: 8.64 us -> 0 us
  matrix products: 5.71 us -> 0 us
  Pallas kernels: 0 us -> 3.22 us
  other arithmetic: 3.72 us -> 2.28 us
    all_to_all x0 -> x1, blocking collectives: none -> 18.3 us  [on_device(): terms = lax.all_to_all(terms, ('xl', 'z'), 0, 0, tiled=True)]
    all_to_all x1 -> x0, starting transfers between devices: 8.94 us -> none  [on_device(): lax.all_to_all(jnp.broadcast_to(terms, (ways, rows)), ('xl', 'z'), 0, 0,...]
    all_to_all x1 -> x0, waiting for transfers between devices: 8.64 us -> none  [on_device(): lax.all_to_all(jnp.broadcast_to(terms, (ways, rows)), ('xl', 'z'), 0, 0,...]
    broadcast_in_dim x3 -> x0, local copies, waits for them, and re-layouts: 8.61 us -> none  [the longest x1 7.75 us: on_device(): jnp.repeat(jnp.repeat(int_map, VTILE, axis=0), VTILE, axis=1)]
    dot_general x1 -> x0, matrix products: 5.71 us -> none  [on_device(): jnp.dot(amp_masked, panel * full_mask, preferred_element_type=jnp.float32)]
    pallas_call x0 -> x1, Pallas kernels: none -> 3.22 us  [on_device(): pl.pallas_call(functools.partial(ladder, (xh, y, c, part)), out_shape=(ja...]
    convert_element_type x3 -> x1, other arithmetic: 2.17 us -> 0.73 us  [on_device(): panel = panel.reshape(y * c * xh, part, columns).astype(jnp.bfloat16)]
    unnamed x3 -> x10, local copies, waits for them, and re-layouts: 3.32 us -> 2.03 us
  transfers between devices with their start and end apart: 1 -> 0, of which waited for: 1 -> 0; matrix products, arithmetic and copies ran while one was open for 1% -> 0% of each run, Pallas kernels for 0% -> 0%
where the time goes in v2:
time: 71.1 us; the launch traced here: 70.9 us
  blocking collectives  62.7 us (88%)
  Pallas kernels  3.22 us (5%)
  other arithmetic  2.28 us (3%)
  local copies, waits for them, and re-layouts  2.03 us (3%)
    all_gather x1, blocking collectives, on_device(): panel = lax.all_gather(pair, ('y', 'c'), axis=0, tiled=False)  38.1 us
    all_to_all x1, blocking collectives, on_device(): terms = lax.all_to_all(terms, ('xl', 'z'), 0, 0, tiled=True)  18.3 us
    all_gather x1, blocking collectives, on_device(): pair = lax.all_gather(mine, 'xh', axis=0, tiled=False)  6.23 us
    pallas_call x1, Pallas kernels, on_device(): pl.pallas_call(functools.partial(ladder, (xh, y, c, part)), out_shape=(ja...  3.22 us
    unnamed x10, local copies, waits for them, and re-layouts  2.03 us

profile of v2, /device:TPU:1, one launch (start us, length us, event | category | flops | bytes accessed | tf_op | source)
XLA Modules:
  0.0 70.9 jit_solution(10047331276979230930)
XLA Ops:
  0.6 0.9 %multiply_convert_fusion = f16[192,256]{1,0:T(8,128)(2,1)S(1)} fusion(bf16[192,256]{1,0:T(8,128)(2,1)} %param.8), kind=kLoop, calls=%fused_computation | loop fusion | flops 147456 | bytes 196608 | tf_op jit(solution)/shard_map/convert_element_type | solution.py:59
  1.6 6.2 %all-gather = f16[384,256]{1,0:T(8,128)(2,1)S(1)} all-gather(f16[192,256]{1,0:T(8,128)(2,1)S(1)} %multiply_convert_fusion), channel_id=2, replica_groups=mesh['xh'=2,'y'=8,'c'=2,'xl'=2,'z'=12] {'xh'}, dimensions={0}, use_global_device_ids=true | all-gather | bytes 294912 | tf_op jit(solution)/shard_map/all_gather | solution.py:60
  7.8 0.0 copy-start.1
  7.8 0.0 copy-start.2
  7.8 0.0 copy-start.3
  7.8 38.1 %all-gather.3 = f16[32,192,256]{2,1,0:T(8,128)(2,1)S(1)} all-gather(f16[2,192,256]{2,1,0:T(8,128)(2,1)S(1)} %bitcast.3), channel_id=3, replica_groups=mesh['xh'=2,'y'=8,'c'=2,'xl'=2,'z'=12] {'y','c'}, dimensions={0}, use_global_device_ids=true | all-gather | bytes 3342336 | tf_op jit(solution)/shard_map/all_gather | solution.py:61
  45.9 0.0 copy-start
  45.9 0.0 copy-start.4
  45.9 0.7 %convert_element_type.15.panel = bf16[32,192,256]{2,1,0:T(8,128)(2,1)S(1)} convert(f16[32,192,256]{2,1,0:T(8,128)(2,1)S(1)} %all-gather.3) | non-fusion elementwise | flops 1572864 | bytes 6291456 | tf_op jit(solution)/shard_map/convert_element_type | solution.py:62
  46.6 0.0 copy-done.1
  46.6 0.0 copy-done.2
  46.7 0.0 copy-done.3
  46.7 2.0 %copy-done = bf16[512,6144]{1,0:T(8,128)(2,1)S(1)} copy-done((bf16[512,6144]{1,0:T(8,128)(2,1)S(1)}, bf16[512,6144]{1,0:T(8,128)(2,1)}, u32[]{:S(2)}) %copy-start) | copy-done | bytes 6291480
  48.7 0.0 copy-done.4
  48.7 3.2 %ladder.1 = (f32[512,256]{1,0:T(8,128)}, f32[24,1,512]{2,1,0:T(1,128)S(1)}) custom-call(s32[8,48]{1,0:T(8,128)S(1)} %copy-done.3, s32[2,48]{1,0:T(2,128)S(1)} %bitcast.2, bf16[512,6144]{1,0:T(8,128)(2,1)S(1)} %copy-done, bf16[32,192,256]{2,1,0:T(8,128)(2,1)S(1)} %convert_element_type.15.panel, bf16[512,256]{1,0:T(8,128)(2,1)S(1)} %copy-done.2, ...), custom_call_target="tpu_custom_call" | custom-call | flops 1610612736 | bytes 6291456 | tf_op jit(solution)/shard_map/ladder/pallas_call | solution.py:64
  51.9 18.3 %all_to_all.5 = f32[24,1,512]{2,1,0:T(1,128)S(1)} all-to-all(f32[24,1,512]{2,1,0:T(1,128)S(1)} %get-tuple-element.5), channel_id=1, replica_groups=mesh['xh'=2,'y'=8,'c'=2,'xl'=2,'z'=12] {'xl','z'}, dimensions={0} | all-to-all | bytes 98304 | tf_op jit(solution)/shard_map/all_to_all | solution.py:78
  70.3 0.6 reduce_sum.9
Async XLA Ops:
  7.8 38.9 %copy-start.1 = (f32[512,256]{1,0:T(8,128)S(1)}, f32[512,256]{1,0:T(8,128)}, u32[]{:S(2)}) copy-start(f32[512,256]{1,0:T(8,128)} %residual_in.1) | copy-start | bytes 1572868
  7.8 38.9 %copy-start.2 = (bf16[512,256]{1,0:T(8,128)(2,1)S(1)}, bf16[512,256]{1,0:T(8,128)(2,1)}, u32[]{:S(2)}) copy-start(bf16[512,256]{1,0:T(8,128)(2,1)} %exchange.1) | copy-start | bytes 786436
  7.8 38.9 %copy-start.3 = (s32[8,48]{1,0:T(8,128)S(1)}, s32[8,48]{1,0:T(8,128)}, u32[]{:S(2)}) copy-start(s32[8,48]{1,0:T(8,128)} %amp_map.1) | copy-start | bytes 4612
  45.9 2.8 %copy-start = (bf16[512,6144]{1,0:T(8,128)(2,1)S(1)}, bf16[512,6144]{1,0:T(8,128)(2,1)}, u32[]{:S(2)}) copy-start(bf16[512,6144]{1,0:T(8,128)(2,1)} %amplitudes.1) | copy-start | bytes 18874372
  45.9 2.8 %copy-start.4 = (s32[48,2]{0,1:T(2,128)S(1)}, s32[48,2]{0,1:T(2,128)}, u32[]{:S(2)}) copy-start(s32[48,2]{0,1:T(2,128)} %param.9) | copy-start | bytes 1156

commit v3 on v2

--- a/solution.py
+++ b/solution.py
@@ -12,14 +12,23 @@
 SCALE = 2.0**19
 
 
-def ladder(shape, amp_map, int_map, amplitudes, panel, exchange, residual_in, residual, terms):
+def ladder(
+    shape, amp_map, int_map, amp_hbm, panel, exchange, residual_in, residual_hbm, terms, amp, residual, in_sems, out_sem
+):
     xh, y, c, part = shape
     rows, columns = residual.shape
     step = 2 * c * part
     chunks = [(h, y0) for h in range(xh) for y0 in range(0, y, 2)]
 
+    def fetch(i):
+        h, y0 = chunks[i]
+        first = (h * y + y0) * c * part
+        return pltpu.make_async_copy(amp_hbm.at[:, first : first + step], amp.at[i], in_sems.at[i])
+
+    for i in range(len(chunks)):
+        fetch(i).start()
     total = jnp.zeros((rows, columns), jnp.float32)
-    for h, y0 in chunks:
+    for i, (h, y0) in enumerate(chunks):
         first = (h * y + y0) * c * part
         right = []
         for at in range(0, step, PTILE):
@@ -31,17 +40,20 @@
                 tiles.append(panel[source, inner : inner + PTILE, j * VTILE : (j + 1) * VTILE] * keep)
             right.append(jnp.concatenate(tiles, axis=1))
         right = jnp.concatenate(right, axis=0)
+        fetch(i).wait()
         left = []
         for r in range(rows // PTILE):
             tiles = []
             for k in range(step // VTILE):
                 keep = amp_map[r, first // VTILE + k].astype(jnp.bfloat16)
-                tiles.append(amplitudes[r * PTILE : (r + 1) * PTILE, first + k * VTILE : first + (k + 1) * VTILE] * keep)
+                tiles.append(amp[i, r * PTILE : (r + 1) * PTILE, k * VTILE : (k + 1) * VTILE] * keep)
             left.append(jnp.concatenate(tiles, axis=1))
         left = jnp.concatenate(left, axis=0)
         total += jnp.dot(left, right, preferred_element_type=jnp.float32)
     total = residual_in[...] + total * (1.0 / SCALE)
     residual[...] = total
+    leave = pltpu.make_async_copy(residual, residual_hbm, out_sem)
+    leave.start()
     product = total * exchange[...].astype(jnp.float32)
     folded = product[:, :VTILE]
     for j in range(1, columns // VTILE):
@@ -49,6 +61,7 @@
     line = jnp.sum(folded.T, axis=0, keepdims=True)
     for i in range(terms.shape[0]):
         terms[i] = line
+    leave.wait()
 
 
 def on_device(amplitudes, amp_map, integrals, int_map, exchange, residual_in):
@@ -56,23 +69,31 @@
     part, depth = integrals.shape[0], amplitudes.shape[1]
     xh, y, c = (lax.axis_size(name) for name in ("xh", "y", "c"))
     ways = lax.axis_size(("xl", "z"))
-    mine = (integrals.astype(jnp.float32) * SCALE).astype(jnp.float16)
-    pair = lax.all_gather(mine, "xh", axis=0, tiled=False)
+    pair = lax.all_gather(integrals, "xh", axis=0, tiled=False)
+    pair = (pair.astype(jnp.float32) * SCALE).astype(jnp.float16)
     panel = lax.all_gather(pair, ("y", "c"), axis=0, tiled=False)
     panel = panel.reshape(y * c * xh, part, columns).astype(jnp.bfloat16)
+    chunks, step = xh * y // 2, 2 * c * part
     vmem, smem = pl.BlockSpec(memory_space=pltpu.VMEM), pl.BlockSpec(memory_space=pltpu.SMEM)
+    anywhere = pl.BlockSpec(memory_space=pl.ANY)
     residual, terms = pl.pallas_call(
         functools.partial(ladder, (xh, y, c, part)),
         out_shape=(
             jax.ShapeDtypeStruct((rows, columns), jnp.float32),
             jax.ShapeDtypeStruct((ways, 1, rows), jnp.float32),
         ),
-        in_specs=[smem, smem, vmem, vmem, vmem, vmem],
-        out_specs=(vmem, vmem),
+        in_specs=[smem, smem, anywhere, vmem, vmem, vmem],
+        out_specs=(anywhere, vmem),
+        scratch_shapes=[
+            pltpu.VMEM((chunks, rows, step), jnp.bfloat16),
+            pltpu.VMEM((rows, columns), jnp.float32),
+            pltpu.SemaphoreType.DMA((chunks,)),
+            pltpu.SemaphoreType.DMA,
+        ],
         cost_estimate=pl.CostEstimate(
             flops=2 * rows * depth * columns, bytes_accessed=2 * rows * depth, transcendentals=0
         ),
-        compiler_params=pltpu.CompilerParams(vmem_limit_bytes=24 << 20),
+        compiler_params=pltpu.CompilerParams(vmem_limit_bytes=50 << 20),
         name="ladder",
     )(amp_map, int_map.T, amplitudes, panel, exchange, residual_in)
     terms = lax.all_to_all(terms, ("xl", "z"), 0, 0, tiled=True)

time: 71.1 us -> 72.2 us (1.015)
  Pallas kernels: 3.22 us -> 6.75 us
  local copies, waits for them, and re-layouts: 2.03 us -> 0.44 us
  other arithmetic: 2.28 us -> 1.34 us
    pallas_call x1, Pallas kernels: 3.22 us -> 6.75 us  [on_device(): pl.pallas_call(functools.partial(ladder, (xh, y, c, part)), out_shape=(ja...]
    unnamed x10 -> x8, local copies, waits for them, and re-layouts: 2.03 us -> 0.44 us
    convert_element_type x1, other arithmetic: 0.92 us -> 0.05 us  [on_device(): pair = (pair.astype(jnp.float32) * SCALE).astype(jnp.float16)]
where the time goes in v3:
time: 72.2 us; the launch traced here: 72 us
  blocking collectives  62.8 us (87%)
  Pallas kernels  6.75 us (9%)
  other arithmetic  1.34 us (2%)
    all_gather x1, blocking collectives, on_device(): panel = lax.all_gather(pair, ('y', 'c'), axis=0, tiled=False)  37.9 us
    all_to_all x1, blocking collectives, on_device(): terms = lax.all_to_all(terms, ('xl', 'z'), 0, 0, tiled=True)  18.4 us
    pallas_call x1, Pallas kernels, on_device(): pl.pallas_call(functools.partial(ladder, (xh, y, c, part)), out_shape=(ja...  6.75 us
    all_gather x1, blocking collectives, on_device(): pair = lax.all_gather(integrals, 'xh', axis=0, tiled=False)  6.51 us

profile of v3, /device:TPU:1, one launch (start us, length us, event | category | flops | bytes accessed | tf_op | source)
XLA Modules:
  0.0 72.0 jit_solution(16162291648782759516)
XLA Ops:
  0.6 6.5 %all-gather = bf16[384,256]{1,0:T(8,128)(2,1)S(1)} all-gather(bf16[192,256]{1,0:T(8,128)(2,1)} %param.8), channel_id=2, replica_groups=mesh['xh'=2,'y'=8,'c'=2,'xl'=2,'z'=12] {'xh'}, dimensions={0}, use_global_device_ids=true | all-gather | bytes 294912 | tf_op jit(solution)/shard_map/all_gather | solution.py:72
  7.2 37.9 %all-gather.3 = f16[32,192,256]{2,1,0:T(8,128)(2,1)S(1)} all-gather(f16[2,192,256]{2,1,0:T(8,128)(2,1)S(1)} %bitcast.3), channel_id=3, replica_groups=mesh['xh'=2,'y'=8,'c'=2,'xl'=2,'z'=12] {'y','c'}, dimensions={0}, use_global_device_ids=true | all-gather | bytes 3342336 | tf_op jit(solution)/shard_map/all_gather | solution.py:74
  45.1 0.0 copy-start
  45.1 0.0 copy-start.1
  45.1 0.0 copy-start.2
  45.1 0.0 copy-start.3
  45.1 0.7 convert_element_type.16.panel
  45.8 0.4 copy-done
  46.2 0.1 copy-done.1
  46.2 0.0 copy-done.2
  46.2 0.0 copy-done.3
  46.2 6.8 %ladder.1 = (f32[512,256]{1,0:T(8,128)}, f32[24,1,512]{2,1,0:T(1,128)S(1)}) custom-call(s32[8,48]{1,0:T(8,128)S(1)} %copy-done.2, s32[2,48]{1,0:T(2,128)S(1)} %bitcast.2, bf16[512,6144]{1,0:T(8,128)(2,1)} %amp_hbm.1, bf16[32,192,256]{2,1,0:T(8,128)(2,1)S(1)} %convert_element_type.16.panel, bf16[512,256]{1,0:T(8,128)(2,1)S(1)} %copy-done.1, ...), custom_call_target="tpu_custom_call" | custom-call | flops 1610612736 | bytes 6291456 | tf_op jit(solution)/shard_map/ladder/pallas_call | solution.py:79
  53.0 18.4 %all_to_all.5 = f32[24,1,512]{2,1,0:T(1,128)S(1)} all-to-all(f32[24,1,512]{2,1,0:T(1,128)S(1)} %get-tuple-element.5), channel_id=1, replica_groups=mesh['xh'=2,'y'=8,'c'=2,'xl'=2,'z'=12] {'xl','z'}, dimensions={0} | all-to-all | bytes 98304 | tf_op jit(solution)/shard_map/all_to_all | solution.py:99
  71.4 0.6 reduce_sum.9
  (1 shorter events, 0.0 us)
Async XLA Ops:
  45.1 1.0 %copy-start = (f32[512,256]{1,0:T(8,128)S(1)}, f32[512,256]{1,0:T(8,128)}, u32[]{:S(2)}) copy-start(f32[512,256]{1,0:T(8,128)} %residual_in.1) | copy-start | bytes 1572868
  45.1 1.1 %copy-start.1 = (bf16[512,256]{1,0:T(8,128)(2,1)S(1)}, bf16[512,256]{1,0:T(8,128)(2,1)}, u32[]{:S(2)}) copy-start(bf16[512,256]{1,0:T(8,128)(2,1)} %exchange.1) | copy-start | bytes 786436
  45.1 1.1 %copy-start.2 = (s32[8,48]{1,0:T(8,128)S(1)}, s32[8,48]{1,0:T(8,128)}, u32[]{:S(2)}) copy-start(s32[8,48]{1,0:T(8,128)} %amp_map.1) | copy-start | bytes 4612
  45.1 1.1 %copy-start.3 = (s32[48,2]{0,1:T(2,128)S(1)}, s32[48,2]{0,1:T(2,128)}, u32[]{:S(2)}) copy-start(s32[48,2]{0,1:T(2,128)} %param.9) | copy-start | bytes 1156

commit v4 on v2

--- a/solution.py
+++ b/solution.py
@@ -56,8 +56,8 @@
     part, depth = integrals.shape[0], amplitudes.shape[1]
     xh, y, c = (lax.axis_size(name) for name in ("xh", "y", "c"))
     ways = lax.axis_size(("xl", "z"))
-    mine = (integrals.astype(jnp.float32) * SCALE).astype(jnp.float16)
-    pair = lax.all_gather(mine, "xh", axis=0, tiled=False)
+    pair = lax.all_gather(integrals, "xh", axis=0, tiled=False)
+    pair = (pair.astype(jnp.float32) * SCALE).astype(jnp.float16)
     panel = lax.all_gather(pair, ("y", "c"), axis=0, tiled=False)
     panel = panel.reshape(y * c * xh, part, columns).astype(jnp.bfloat16)
     vmem, smem = pl.BlockSpec(memory_space=pltpu.VMEM), pl.BlockSpec(memory_space=pltpu.SMEM)

time: 71.1 us -> 70.5 us (level)
  other arithmetic: 2.28 us -> 1.41 us
    convert_element_type x1, other arithmetic: 0.92 us -> 0.05 us  [on_device(): pair = (pair.astype(jnp.float32) * SCALE).astype(jnp.float16)]
where the time goes in v4:
time: 70.5 us; the launch traced here: 70.3 us
  blocking collectives  62.9 us (89%)
  Pallas kernels  3.22 us (5%)
  local copies, waits for them, and re-layouts  2.04 us (3%)
  other arithmetic  1.41 us (2%)
    all_gather x1, blocking collectives, on_device(): panel = lax.all_gather(pair, ('y', 'c'), axis=0, tiled=False)  38.1 us
    all_to_all x1, blocking collectives, on_device(): terms = lax.all_to_all(terms, ('xl', 'z'), 0, 0, tiled=True)  18.4 us
    all_gather x1, blocking collectives, on_device(): pair = lax.all_gather(integrals, 'xh', axis=0, tiled=False)  6.51 us
    pallas_call x1, Pallas kernels, on_device(): pl.pallas_call(functools.partial(ladder, (xh, y, c, part)), out_shape=(ja...  3.22 us
    unnamed x10, local copies, waits for them, and re-layouts  2.04 us

profile of v4, /device:TPU:1, one launch (start us, length us, event | category | flops | bytes accessed | tf_op | source)
XLA Modules:
  0.0 70.3 jit_solution(16183067346554796597)
XLA Ops:
  0.6 6.5 %all-gather = bf16[384,256]{1,0:T(8,128)(2,1)S(1)} all-gather(bf16[192,256]{1,0:T(8,128)(2,1)} %param.8), channel_id=2, replica_groups=mesh['xh'=2,'y'=8,'c'=2,'xl'=2,'z'=12] {'xh'}, dimensions={0}, use_global_device_ids=true | all-gather | bytes 294912 | tf_op jit(solution)/shard_map/all_gather | solution.py:59
  7.2 0.0 copy-start.1
  7.2 0.0 copy-start.2
  7.2 0.0 copy-start.3
  7.2 38.1 %all-gather.3 = f16[32,192,256]{2,1,0:T(8,128)(2,1)S(1)} all-gather(f16[2,192,256]{2,1,0:T(8,128)(2,1)S(1)} %bitcast.3), channel_id=3, replica_groups=mesh['xh'=2,'y'=8,'c'=2,'xl'=2,'z'=12] {'y','c'}, dimensions={0}, use_global_device_ids=true | all-gather | bytes 3342336 | tf_op jit(solution)/shard_map/all_gather | solution.py:61
  45.3 0.0 copy-start
  45.3 0.0 copy-start.4
  45.3 0.7 %convert_element_type.16.panel = bf16[32,192,256]{2,1,0:T(8,128)(2,1)S(1)} convert(f16[32,192,256]{2,1,0:T(8,128)(2,1)S(1)} %all-gather.3) | non-fusion elementwise | flops 1572864 | bytes 6291456 | tf_op jit(solution)/shard_map/convert_element_type | solution.py:62
  46.0 0.0 copy-done.1
  46.0 0.0 copy-done.2
  46.1 0.0 copy-done.3
  46.1 2.0 %copy-done = bf16[512,6144]{1,0:T(8,128)(2,1)S(1)} copy-done((bf16[512,6144]{1,0:T(8,128)(2,1)S(1)}, bf16[512,6144]{1,0:T(8,128)(2,1)}, u32[]{:S(2)}) %copy-start) | copy-done | bytes 6291480
  48.1 0.0 copy-done.4
  48.1 3.2 %ladder.1 = (f32[512,256]{1,0:T(8,128)}, f32[24,1,512]{2,1,0:T(1,128)S(1)}) custom-call(s32[8,48]{1,0:T(8,128)S(1)} %copy-done.3, s32[2,48]{1,0:T(2,128)S(1)} %bitcast.2, bf16[512,6144]{1,0:T(8,128)(2,1)S(1)} %copy-done, bf16[32,192,256]{2,1,0:T(8,128)(2,1)S(1)} %convert_element_type.16.panel, bf16[512,256]{1,0:T(8,128)(2,1)S(1)} %copy-done.2, ...), custom_call_target="tpu_custom_call" | custom-call | flops 1610612736 | bytes 6291456 | tf_op jit(solution)/shard_map/ladder/pallas_call | solution.py:64
  51.3 18.4 %all_to_all.5 = f32[24,1,512]{2,1,0:T(1,128)S(1)} all-to-all(f32[24,1,512]{2,1,0:T(1,128)S(1)} %get-tuple-element.5), channel_id=1, replica_groups=mesh['xh'=2,'y'=8,'c'=2,'xl'=2,'z'=12] {'xl','z'}, dimensions={0} | all-to-all | bytes 98304 | tf_op jit(solution)/shard_map/all_to_all | solution.py:78
  69.7 0.6 reduce_sum.9
  (1 shorter events, 0.0 us)
Async XLA Ops:
  7.2 38.8 %copy-start.1 = (f32[512,256]{1,0:T(8,128)S(1)}, f32[512,256]{1,0:T(8,128)}, u32[]{:S(2)}) copy-start(f32[512,256]{1,0:T(8,128)} %residual_in.1) | copy-start | bytes 1572868
  7.2 38.8 %copy-start.2 = (bf16[512,256]{1,0:T(8,128)(2,1)S(1)}, bf16[512,256]{1,0:T(8,128)(2,1)}, u32[]{:S(2)}) copy-start(bf16[512,256]{1,0:T(8,128)(2,1)} %exchange.1) | copy-start | bytes 786436
  7.2 38.8 %copy-start.3 = (s32[8,48]{1,0:T(8,128)S(1)}, s32[8,48]{1,0:T(8,128)}, u32[]{:S(2)}) copy-start(s32[8,48]{1,0:T(8,128)} %amp_map.1) | copy-start | bytes 4612
  45.3 2.8 %copy-start = (bf16[512,6144]{1,0:T(8,128)(2,1)S(1)}, bf16[512,6144]{1,0:T(8,128)(2,1)}, u32[]{:S(2)}) copy-start(bf16[512,6144]{1,0:T(8,128)(2,1)} %amplitudes.1) | copy-start | bytes 18874372
  45.3 2.8 %copy-start.4 = (s32[48,2]{0,1:T(2,128)S(1)}, s32[48,2]{0,1:T(2,128)}, u32[]{:S(2)}) copy-start(s32[48,2]{0,1:T(2,128)} %param.9) | copy-start | bytes 1156

commit v5 on v4

v5 whole, which is shorter than its diff:
```python
import functools

import jax
import jax.numpy as jnp
from jax import lax
from jax.experimental import pallas as pl
from jax.experimental.pallas import tpu as pltpu
from jax.sharding import Mesh, PartitionSpec as P

PTILE = 64
VTILE = 128
EARLY = 6
SCALE = 2.0**19


def multiply(shape, start, amp_map, int_map, amplitudes, panel):
    xh, y, c, part = shape
    rows, columns = amplitudes.shape[0], panel.shape[2]
    step = 2 * c * part
    total = jnp.zeros((rows, columns), jnp.float32)
    for h, y0 in [(h, y0) for h in range(xh) for y0 in range(0, panel.shape[0] // (c * xh), 2)]:
        first = (h * y + start + y0) * c * part
        right = []
        for at in range(0, step, PTILE):
            block, inner = divmod(at, part)
            source = ((y0 + block // c) * c + block % c) * xh + h
            tiles = []
            for j in range(columns // VTILE):
                keep = int_map[j, (first + at) // VTILE].astype(jnp.bfloat16)
                tiles.append(panel[source, inner : inner + PTILE, j * VTILE : (j + 1) * VTILE] * keep)
            right.append(jnp.concatenate(tiles, axis=1))
        right = jnp.concatenate(right, axis=0)
        left = []
        for r in range(rows // PTILE):
            tiles = []
            for k in range(step // VTILE):
                keep = amp_map[r, first // VTILE + k].astype(jnp.bfloat16)
                at = first + k * VTILE
                tiles.append(amplitudes[r * PTILE : (r + 1) * PTILE, at : at + VTILE] * keep)
            left.append(jnp.concatenate(tiles, axis=1))
        left = jnp.concatenate(left, axis=0)
        total += jnp.dot(left, right, preferred_element_type=jnp.float32)
    return total * (1.0 / SCALE)


def opening(shape, start, amp_map, int_map, amplitudes, panel, partial):
    partial[...] = multiply(shape, start, amp_map, int_map, amplitudes, panel)


def closing(
    shape, start, amp_map, int_map, amplitudes, panel, partial, residual_in, exchange, residual_hbm, terms, residual, sem
):
    total = residual_in[...] + (partial[...] + multiply(shape, start, amp_map, int_map, amplitudes, panel))
    residual[...] = total
    leave = pltpu.make_async_copy(residual, residual_hbm, sem)
    leave.start()
    product = total * exchange[...].astype(jnp.float32)
    folded = product[:, :VTILE]
    for j in range(1, product.shape[1] // VTILE):
        folded += product[:, j * VTILE : (j + 1) * VTILE]
    line = jnp.sum(folded.T, axis=0, keepdims=True)
    for i in range(terms.shape[0]):
        terms[i] = line
    leave.wait()


def on_device(amplitudes, amp_map, integrals, int_map, exchange, residual_in):
    rows, columns = residual_in.shape
    part, depth = integrals.shape[0], amplitudes.shape[1]
    xh, y, c = (lax.axis_size(name) for name in ("xh", "y", "c"))
    ways = lax.axis_size(("xl", "z"))
    pair = lax.all_gather(integrals, "xh", axis=0, tiled=False)
    pair = (pair.astype(jnp.float32) * SCALE).astype(jnp.float16)
    panel = lax.all_gather(pair, ("y", "c"), axis=0, tiled=False)
    panel = panel.reshape(y * c * xh, part, columns)
    vmem, smem = pl.BlockSpec(memory_space=pltpu.VMEM), pl.BlockSpec(memory_space=pltpu.SMEM)

    def call(body, start, stop, outs, specs, others, scratch=()):
        share = depth * (stop - start) // y
        return pl.pallas_call(
            functools.partial(body, (xh, y, c, part), start),
            out_shape=outs,
            in_specs=[smem, smem, vmem, vmem] + [vmem] * len(others),
            out_specs=specs,
            scratch_shapes=scratch,
            cost_estimate=pl.CostEstimate(
                flops=2 * rows * share * columns, bytes_accessed=2 * rows * share, transcendentals=0
            ),
            compiler_params=pltpu.CompilerParams(vmem_limit_bytes=24 << 20),
            name=body.__name__,
        )(amp_map, int_map.T, amplitudes, panel[start * c * xh : stop * c * xh].astype(jnp.bfloat16), *others)

    block = jax.ShapeDtypeStruct((rows, columns), jnp.float32)
    lines = jax.ShapeDtypeStruct((ways, 1, rows), jnp.float32)
    partial = call(opening, 0, EARLY, block, vmem, ())
    partial, panel = lax.optimization_barrier((partial, panel))
    residual, terms = call(
        closing,
        EARLY,
        y,
        (block, lines),
        (pl.BlockSpec(memory_space=pl.ANY), vmem),
        (partial, residual_in, exchange),
        [pltpu.VMEM((rows, columns), jnp.float32), pltpu.SemaphoreType.DMA],
    )
    terms = lax.all_to_all(terms, ("xl", "z"), 0, 0, tiled=True)
    return residual, jnp.sum(terms, axis=(0, 1))


def solution(mesh):
    fine = Mesh(mesh.devices.reshape(2, 8, 2, 2, 12), ("xh", "y", "c", "xl", "z"))
    occ, virt = ("xh", "y", "c"), ("xl", "z")
    in_specs = (P(occ, None), P(occ, None), P(occ, virt), P(None, virt), P(occ, virt), P(occ, virt))
    return jax.shard_map(on_device, mesh=fine, in_specs=in_specs, out_specs=(P(occ, virt), P(occ)), check_vma=False)
```

time: 70.5 us -> 69.4 us (0.984)
  local copies, waits for them, and re-layouts: 2.04 us -> 0.13 us
  Pallas kernels: 3.22 us -> 4.04 us
    unnamed x10, local copies, waits for them, and re-layouts: 2.04 us -> 0.13 us
    pallas_call x1 -> x2, Pallas kernels: 3.22 us -> 4.04 us  [call(): pl.pallas_call(functools.partial(body, (xh, y, c, part), start), out_shap...]
where the time goes in v5:
time: 69.4 us; the launch traced here: 69.2 us
  blocking collectives  62.9 us (91%)
  Pallas kernels  4.04 us (6%)
  other arithmetic  1.38 us (2%)
  between operations  0.7 us (1%)
    all_gather x1, blocking collectives, on_device(): panel = lax.all_gather(pair, ('y', 'c'), axis=0, tiled=False)  38.1 us
    all_to_all x1, blocking collectives, on_device(): terms = lax.all_to_all(terms, ('xl', 'z'), 0, 0, tiled=True)  18.4 us
    all_gather x1, blocking collectives, on_device(): pair = lax.all_gather(integrals, 'xh', axis=0, tiled=False)  6.51 us
    pallas_call x2, Pallas kernels, call(): pl.pallas_call(functools.partial(body, (xh, y, c, part), start), out_shap...  4.04 us

profile of v5, /device:TPU:1, one launch (start us, length us, event | category | flops | bytes accessed | tf_op | source)
XLA Modules:
  0.0 69.2 jit_solution(6936731894743904312)
XLA Ops:
  0.6 6.5 %all-gather = bf16[384,256]{1,0:T(8,128)(2,1)S(1)} all-gather(bf16[192,256]{1,0:T(8,128)(2,1)} %param.8), channel_id=2, replica_groups=mesh['xh'=2,'y'=8,'c'=2,'xl'=2,'z'=12] {'xh'}, dimensions={0}, use_global_device_ids=true | all-gather | bytes 294912 | tf_op jit(solution)/shard_map/all_gather | solution.py:72
  7.2 0.0 copy-start
  7.2 38.1 %all-gather.3 = f16[32,192,256]{2,1,0:T(8,128)(2,1)S(1)} all-gather(f16[2,192,256]{2,1,0:T(8,128)(2,1)S(1)} %bitcast.4), channel_id=3, replica_groups=mesh['xh'=2,'y'=8,'c'=2,'xl'=2,'z'=12] {'y','c'}, dimensions={0}, use_global_device_ids=true | all-gather | bytes 3342336 | tf_op jit(solution)/shard_map/all_gather | solution.py:74
  45.3 0.0 copy-start.3
  45.3 0.0 copy-start.4
  45.3 0.6 slice_convert_fusion.panel
  45.8 0.0 copy-done
  45.8 0.1 copy-done.3
  46.0 0.0 copy-done.4
  46.0 0.0 copy-start.1
  46.0 0.0 copy-start.2
  46.0 2.0 %opening.1.partial = f32[512,256]{1,0:T(8,128)S(1)} custom-call(s32[8,48]{1,0:T(8,128)S(1)} %copy-done.3, s32[2,48]{1,0:T(2,128)S(1)} %bitcast.2, bf16[512,6144]{1,0:T(8,128)(2,1)S(1)} %copy-done, bf16[24,192,256]{2,1,0:T(8,128)(2,1)S(1)} %slice_convert_fusion.panel), custom_call_target="tpu_custom_call" | custom-call | flops 1207959552 | bytes 4718592 | tf_op jit(solution)/shard_map/opening/pallas_call | solution.py:80
  48.0 0.1 slice_convert_fusion.1.panel
  48.1 0.0 copy-done.1
  48.2 0.0 copy-done.2
  48.2 2.0 %closing.1 = (f32[512,256]{1,0:T(8,128)}, f32[24,1,512]{2,1,0:T(1,128)S(1)}) custom-call(s32[8,48]{1,0:T(8,128)S(1)} %copy-done.3, s32[2,48]{1,0:T(2,128)S(1)} %bitcast.3, bf16[512,6144]{1,0:T(8,128)(2,1)S(1)} %copy-done, bf16[8,192,256]{2,1,0:T(8,128)(2,1)S(1)} %slice_convert_fusion.1.panel, f32[512,256]{1,0:T(8,128)S(1)} %opening.1.partial, ...), custom_call_target="tpu_custom_call" | custom-call | flops 402653184 | bytes 1572864 | tf_op jit(solution)/shard_map/closing/pallas_call | solution.py:80
  50.2 18.4 %all_to_all.5 = f32[24,1,512]{2,1,0:T(1,128)S(1)} all-to-all(f32[24,1,512]{2,1,0:T(1,128)S(1)} %get-tuple-element.9), channel_id=1, replica_groups=mesh['xh'=2,'y'=8,'c'=2,'xl'=2,'z'=12] {'xl','z'}, dimensions={0} | all-to-all | bytes 98304 | tf_op jit(solution)/shard_map/all_to_all | solution.py:106
  68.6 0.6 reduce_sum.9
  (1 shorter events, 0.0 us)
Async XLA Ops:
  7.2 38.6 %copy-start = (bf16[512,6144]{1,0:T(8,128)(2,1)S(1)}, bf16[512,6144]{1,0:T(8,128)(2,1)}, u32[]{:S(2)}) copy-start(bf16[512,6144]{1,0:T(8,128)(2,1)} %amplitudes.3) | copy-start | bytes 18874372
  45.3 0.7 copy-start.3
  45.3 0.7 %copy-start.4 = (s32[48,2]{0,1:T(2,128)S(1)}, s32[48,2]{0,1:T(2,128)}, u32[]{:S(2)}) copy-start(s32[48,2]{0,1:T(2,128)} %param.9) | copy-start | bytes 1156
  46.0 2.2 %copy-start.1 = (f32[512,256]{1,0:T(8,128)S(1)}, f32[512,256]{1,0:T(8,128)}, u32[]{:S(2)}) copy-start(f32[512,256]{1,0:T(8,128)} %residual_in.1) | copy-start | bytes 1572868
  46.0 2.2 %copy-start.2 = (bf16[512,256]{1,0:T(8,128)(2,1)S(1)}, bf16[512,256]{1,0:T(8,128)(2,1)}, u32[]{:S(2)}) copy-start(bf16[512,256]{1,0:T(8,128)(2,1)} %exchange.1) | copy-start | bytes 786436

commit v6 on v4

v6 whole, which is shorter than its diff:
```python
import functools

import jax
import jax.numpy as jnp
from jax import lax
from jax.experimental import pallas as pl
from jax.experimental.pallas import tpu as pltpu
from jax.sharding import Mesh, PartitionSpec as P

PTILE = 64
VTILE = 128
EARLY = 4
SCALE = 2.0**19


def touch(amplitudes, near, residual_in, exchange, token):
    token[...] = amplitudes[: token.shape[0], : token.shape[1]]


def ladder(
    shape, amp_map, int_map, amplitudes, near, far, token, residual_in, exchange, residual_hbm, terms, residual, sems
):
    xh, y, c, part = shape
    rows, columns = residual.shape
    step = 2 * c * part
    total = jnp.zeros((rows, columns), jnp.float32)
    for panel, start in ((near, 0), (far, EARLY)):
        for h, y0 in [(h, y0) for h in range(xh) for y0 in range(0, panel.shape[0] // (c * xh), 2)]:
            first = (h * y + start + y0) * c * part
            right = []
            for at in range(0, step, PTILE):
                block, inner = divmod(at, part)
                source = ((y0 + block // c) * c + block % c) * xh + h
                tiles = []
                for j in range(columns // VTILE):
                    keep = int_map[j, (first + at) // VTILE].astype(jnp.bfloat16)
                    tiles.append(panel[source, inner : inner + PTILE, j * VTILE : (j + 1) * VTILE] * keep)
                right.append(jnp.concatenate(tiles, axis=1))
            right = jnp.concatenate(right, axis=0)
            left = []
            for r in range(rows // PTILE):
                tiles = []
                for k in range(step // VTILE):
                    keep = amp_map[r, first // VTILE + k].astype(jnp.bfloat16)
                    at = first + k * VTILE
                    tiles.append(amplitudes[r * PTILE : (r + 1) * PTILE, at : at + VTILE] * keep)
                left.append(jnp.concatenate(tiles, axis=1))
            left = jnp.concatenate(left, axis=0)
            total += jnp.dot(left, right, preferred_element_type=jnp.float32)
    total = residual_in[...] + total * (1.0 / SCALE)
    some = rows // sems.shape[0]
    leaving = []
    for i in range(sems.shape[0]):
        block = pl.ds(i * some, some)
        residual[block] = total[i * some : (i + 1) * some]
        leaving.append(pltpu.make_async_copy(residual.at[block], residual_hbm.at[block], sems.at[i]))
        leaving[-1].start()
    product = total * exchange[...].astype(jnp.float32)
    folded = product[:, :VTILE]
    for j in range(1, columns // VTILE):
        folded += product[:, j * VTILE : (j + 1) * VTILE]
    line = jnp.sum(folded.T, axis=0, keepdims=True)
    for i in range(terms.shape[0]):
        terms[i] = line
    for copy in leaving:
        copy.wait()


def on_device(amplitudes, amp_map, integrals, int_map, exchange, residual_in):
    rows, columns = residual_in.shape
    part, depth = integrals.shape[0], amplitudes.shape[1]
    xh, y, c = (lax.axis_size(name) for name in ("xh", "y", "c"))
    ways = lax.axis_size(("xl", "z"))
    pair = lax.all_gather(integrals, "xh", axis=0, tiled=False)
    pair = (pair.astype(jnp.float32) * SCALE).astype(jnp.float16)
    panel = lax.all_gather(pair, ("y", "c"), axis=0, tiled=False)
    panel = panel.reshape(y * c * xh, part, columns)
    vmem, smem = pl.BlockSpec(memory_space=pltpu.VMEM), pl.BlockSpec(memory_space=pltpu.SMEM)

    cut = EARLY * c * xh
    near = panel[:cut].astype(jnp.bfloat16)
    token = pl.pallas_call(
        touch,
        out_shape=jax.ShapeDtypeStruct((16, VTILE), amplitudes.dtype),
        in_specs=[vmem] * 4,
        out_specs=vmem,
        compiler_params=pltpu.CompilerParams(vmem_limit_bytes=4 << 20),
        name="touch",
    )(amplitudes, near, residual_in, exchange)
    near, token, panel = lax.optimization_barrier((near, token, panel))
    far = panel[cut:].astype(jnp.bfloat16)
    residual, terms = pl.pallas_call(
        functools.partial(ladder, (xh, y, c, part)),
        out_shape=(
            jax.ShapeDtypeStruct((rows, columns), jnp.float32),
            jax.ShapeDtypeStruct((ways, 1, rows), jnp.float32),
        ),
        in_specs=[smem, smem] + [vmem] * 6,
        out_specs=(pl.BlockSpec(memory_space=pl.ANY), vmem),
        scratch_shapes=[pltpu.VMEM((rows, columns), jnp.float32), pltpu.SemaphoreType.DMA((4,))],
        cost_estimate=pl.CostEstimate(
            flops=2 * rows * depth * columns, bytes_accessed=2 * rows * depth, transcendentals=0
        ),
        compiler_params=pltpu.CompilerParams(vmem_limit_bytes=24 << 20),
        name="ladder",
    )(amp_map, int_map.T, amplitudes, near, far, token, residual_in, exchange)
    terms = lax.all_to_all(terms, ("xl", "z"), 0, 0, tiled=True)
    return residual, jnp.sum(terms, axis=(0, 1))


def solution(mesh):
    fine = Mesh(mesh.devices.reshape(2, 8, 2, 2, 12), ("xh", "y", "c", "xl", "z"))
    occ, virt = ("xh", "y", "c"), ("xl", "z")
    in_specs = (P(occ, None), P(occ, None), P(occ, virt), P(None, virt), P(occ, virt), P(occ, virt))
    return jax.shard_map(on_device, mesh=fine, in_specs=in_specs, out_specs=(P(occ, virt), P(occ)), check_vma=False)
```

time: 70.5 us -> 68.9 us (0.977)
  local copies, waits for them, and re-layouts: 2.04 us -> 0.37 us
    unnamed x10, local copies, waits for them, and re-layouts: 2.04 us -> 0.37 us
where the time goes in v6:
time: 68.9 us; the launch traced here: 68.7 us
  blocking collectives  63.1 us (92%)
  Pallas kernels  3.18 us (5%)
  other arithmetic  1.32 us (2%)
  between operations  0.72 us (1%)
    all_gather x1, blocking collectives, on_device(): panel = lax.all_gather(pair, ('y', 'c'), axis=0, tiled=False)  38.1 us
    all_to_all x1, blocking collectives, on_device(): terms = lax.all_to_all(terms, ('xl', 'z'), 0, 0, tiled=True)  18.4 us
    all_gather x1, blocking collectives, on_device(): pair = lax.all_gather(integrals, 'xh', axis=0, tiled=False)  6.64 us
    pallas_call x1, Pallas kernels, on_device(): pl.pallas_call(functools.partial(ladder, (xh, y, c, part)), out_shape=(ja...  3.18 us

profile of v6, /device:TPU:1, one launch (start us, length us, event | category | flops | bytes accessed | tf_op | source)
XLA Modules:
  0.0 68.7 jit_solution(5729807675195311522)
XLA Ops:
  0.6 0.0 copy-start.2
  0.6 6.6 %all-gather = bf16[384,256]{1,0:T(8,128)(2,1)S(1)} all-gather(bf16[192,256]{1,0:T(8,128)(2,1)} %param.8), channel_id=2, replica_groups=mesh['xh'=2,'y'=8,'c'=2,'xl'=2,'z'=12] {'xh'}, dimensions={0}, use_global_device_ids=true | all-gather | bytes 294912 | tf_op jit(solution)/shard_map/all_gather | solution.py:74
  7.3 0.0 copy-start.1
  7.3 0.0 copy-start
  7.3 38.1 %all-gather.3 = f16[32,192,256]{2,1,0:T(8,128)(2,1)S(1)} all-gather(f16[2,192,256]{2,1,0:T(8,128)(2,1)S(1)} %bitcast.3), channel_id=3, replica_groups=mesh['xh'=2,'y'=8,'c'=2,'xl'=2,'z'=12] {'y','c'}, dimensions={0}, use_global_device_ids=true | all-gather | bytes 3342336 | tf_op jit(solution)/shard_map/all_gather | solution.py:76
  45.4 0.3 slice_convert_fusion.near
  45.7 0.0 copy-done.2
  45.7 0.0 copy-done.1
  45.8 0.0 copy-done
  45.8 0.0 copy-start.3
  45.8 0.0 copy-start.4
  45.8 0.3 slice_convert_fusion.1.far
  46.1 0.3 copy-done.3
  46.5 0.0 copy-done.4
  46.5 3.2 %ladder.1 = (f32[512,256]{1,0:T(8,128)}, f32[24,1,512]{2,1,0:T(1,128)S(1)}) custom-call(s32[8,48]{1,0:T(8,128)S(1)} %copy-done.3, s32[2,48]{1,0:T(2,128)S(1)} %bitcast.2, bf16[512,6144]{1,0:T(8,128)(2,1)S(1)} %copy-done, bf16[16,192,256]{2,1,0:T(8,128)(2,1)S(1)} %slice_convert_fusion.near, bf16[16,192,256]{2,1,0:T(8,128)(2,1)S(1)} %slice_convert_fusion.1.far, ...), custom_call_target="tpu_custom_call" | custom-call | flops 1610612736 | bytes 6291456 | tf_op jit(solution)/shard_map/ladder/pallas_call | solution.py:92
  49.7 18.4 %all_to_all.5 = f32[24,1,512]{2,1,0:T(1,128)S(1)} all-to-all(f32[24,1,512]{2,1,0:T(1,128)S(1)} %get-tuple-element.11), channel_id=1, replica_groups=mesh['xh'=2,'y'=8,'c'=2,'xl'=2,'z'=12] {'xl','z'}, dimensions={0} | all-to-all | bytes 98304 | tf_op jit(solution)/shard_map/all_to_all | solution.py:107
  68.0 0.6 reduce_sum.9
  (2 shorter events, 0.1 us)
Async XLA Ops:
  0.6 45.1 %copy-start.2 = (bf16[512,256]{1,0:T(8,128)(2,1)S(1)}, bf16[512,256]{1,0:T(8,128)(2,1)}, u32[]{:S(2)}) copy-start(bf16[512,256]{1,0:T(8,128)(2,1)} %exchange.3) | copy-start | bytes 786436
  7.3 38.5 %copy-start.1 = (f32[512,256]{1,0:T(8,128)S(1)}, f32[512,256]{1,0:T(8,128)}, u32[]{:S(2)}) copy-start(f32[512,256]{1,0:T(8,128)} %residual_in.3) | copy-start | bytes 1572868
  7.3 38.4 %copy-start = (bf16[512,6144]{1,0:T(8,128)(2,1)S(1)}, bf16[512,6144]{1,0:T(8,128)(2,1)}, u32[]{:S(2)}) copy-start(bf16[512,6144]{1,0:T(8,128)(2,1)} %amplitudes.3) | copy-start | bytes 18874372
  45.8 0.7 %copy-start.3 = (s32[8,48]{1,0:T(8,128)S(1)}, s32[8,48]{1,0:T(8,128)}, u32[]{:S(2)}) copy-start(s32[8,48]{1,0:T(8,128)} %amp_map.1) | copy-start | bytes 4612
  45.8 0.7 copy-start.4

commit v7 on v6

--- a/solution.py
+++ b/solution.py
@@ -13,7 +13,7 @@
 SCALE = 2.0**19
 
 
-def touch(amplitudes, near, residual_in, exchange, token):
+def touch(amplitudes, near, residual_in, exchange, amp_map, int_map, token):
     token[...] = amplitudes[: token.shape[0], : token.shape[1]]
 
 
@@ -82,11 +82,11 @@
     token = pl.pallas_call(
         touch,
         out_shape=jax.ShapeDtypeStruct((16, VTILE), amplitudes.dtype),
-        in_specs=[vmem] * 4,
+        in_specs=[vmem] * 6,
         out_specs=vmem,
         compiler_params=pltpu.CompilerParams(vmem_limit_bytes=4 << 20),
         name="touch",
-    )(amplitudes, near, residual_in, exchange)
+    )(amplitudes, near, residual_in, exchange, amp_map, int_map.T)
     near, token, panel = lax.optimization_barrier((near, token, panel))
     far = panel[cut:].astype(jnp.bfloat16)
     residual, terms = pl.pallas_call(

time: 68.9 us -> 68.8 us (level)
  no operation moved by 1% of the time
where the time goes in v7:
time: 68.8 us; the launch traced here: 68.6 us
  blocking collectives  63.1 us (92%)
  Pallas kernels  3.18 us (5%)
  other arithmetic  1.32 us (2%)
  between operations  0.7 us (1%)
    all_gather x1, blocking collectives, on_device(): panel = lax.all_gather(pair, ('y', 'c'), axis=0, tiled=False)  38.1 us
    all_to_all x1, blocking collectives, on_device(): terms = lax.all_to_all(terms, ('xl', 'z'), 0, 0, tiled=True)  18.4 us
    all_gather x1, blocking collectives, on_device(): pair = lax.all_gather(integrals, 'xh', axis=0, tiled=False)  6.64 us
    pallas_call x1, Pallas kernels, on_device(): pl.pallas_call(functools.partial(ladder, (xh, y, c, part)), out_shape=(ja...  3.18 us

profile of v7, /device:TPU:1, one launch (start us, length us, event | category | flops | bytes accessed | tf_op | source)
XLA Modules:
  0.0 68.6 jit_solution(12795581837266136631)
XLA Ops:
  0.6 0.0 copy-start.2
  0.6 6.6 %all-gather = bf16[384,256]{1,0:T(8,128)(2,1)S(1)} all-gather(bf16[192,256]{1,0:T(8,128)(2,1)} %param.8), channel_id=2, replica_groups=mesh['xh'=2,'y'=8,'c'=2,'xl'=2,'z'=12] {'xh'}, dimensions={0}, use_global_device_ids=true | all-gather | bytes 294912 | tf_op jit(solution)/shard_map/all_gather | solution.py:74
  7.3 0.0 copy-start.1
  7.3 0.0 copy-start
  7.3 38.1 %all-gather.3 = f16[32,192,256]{2,1,0:T(8,128)(2,1)S(1)} all-gather(f16[2,192,256]{2,1,0:T(8,128)(2,1)S(1)} %bitcast.4), channel_id=3, replica_groups=mesh['xh'=2,'y'=8,'c'=2,'xl'=2,'z'=12] {'y','c'}, dimensions={0}, use_global_device_ids=true | all-gather | bytes 3342336 | tf_op jit(solution)/shard_map/all_gather | solution.py:76
  45.4 0.0 copy-start.3
  45.4 0.0 copy-start.4
  45.4 0.3 slice_convert_fusion.near
  45.7 0.0 copy-done.2
  45.8 0.0 copy-done.1
  45.8 0.0 copy-done
  45.8 0.3 copy-done.3
  46.1 0.0 copy-done.4
  46.1 0.3 slice_convert_fusion.1.far
  46.4 3.2 %ladder.1 = (f32[512,256]{1,0:T(8,128)}, f32[24,1,512]{2,1,0:T(1,128)S(1)}) custom-call(s32[8,48]{1,0:T(8,128)S(1)} %copy-done.3, s32[2,48]{1,0:T(2,128)S(1)} %bitcast.3, bf16[512,6144]{1,0:T(8,128)(2,1)S(1)} %copy-done, bf16[16,192,256]{2,1,0:T(8,128)(2,1)S(1)} %slice_convert_fusion.near, bf16[16,192,256]{2,1,0:T(8,128)(2,1)S(1)} %slice_convert_fusion.1.far, ...), custom_call_target="tpu_custom_call" | custom-call | flops 1610612736 | bytes 6291456 | tf_op jit(solution)/shard_map/ladder/pallas_call | solution.py:92
  49.6 18.4 %all_to_all.5 = f32[24,1,512]{2,1,0:T(1,128)S(1)} all-to-all(f32[24,1,512]{2,1,0:T(1,128)S(1)} %get-tuple-element.11), channel_id=1, replica_groups=mesh['xh'=2,'y'=8,'c'=2,'xl'=2,'z'=12] {'xl','z'}, dimensions={0} | all-to-all | bytes 98304 | tf_op jit(solution)/shard_map/all_to_all | solution.py:107
  68.0 0.6 reduce_sum.9
  (2 shorter events, 0.1 us)
Async XLA Ops:
  0.6 45.1 %copy-start.2 = (bf16[512,256]{1,0:T(8,128)(2,1)S(1)}, bf16[512,256]{1,0:T(8,128)(2,1)}, u32[]{:S(2)}) copy-start(bf16[512,256]{1,0:T(8,128)(2,1)} %exchange.3) | copy-start | bytes 786436
  7.3 38.5 %copy-start.1 = (f32[512,256]{1,0:T(8,128)S(1)}, f32[512,256]{1,0:T(8,128)}, u32[]{:S(2)}) copy-start(f32[512,256]{1,0:T(8,128)} %residual_in.3) | copy-start | bytes 1572868
  7.3 38.4 %copy-start = (bf16[512,6144]{1,0:T(8,128)(2,1)S(1)}, bf16[512,6144]{1,0:T(8,128)(2,1)}, u32[]{:S(2)}) copy-start(bf16[512,6144]{1,0:T(8,128)(2,1)} %amplitudes.3) | copy-start | bytes 18874372
  45.4 0.7 %copy-start.3 = (s32[8,48]{1,0:T(8,128)S(1)}, s32[8,48]{1,0:T(8,128)}, u32[]{:S(2)}) copy-start(s32[8,48]{1,0:T(8,128)} %amp_map.3) | copy-start | bytes 4612
  45.4 0.7 %copy-start.4 = (s32[48,2]{0,1:T(2,128)S(1)}, s32[48,2]{0,1:T(2,128)}, u32[]{:S(2)}) copy-start(s32[48,2]{0,1:T(2,128)} %param.9) | copy-start | bytes 1156

commit v8 on v6

--- a/solution.py
+++ b/solution.py
@@ -97,7 +97,7 @@
         ),
         in_specs=[smem, smem] + [vmem] * 6,
         out_specs=(pl.BlockSpec(memory_space=pl.ANY), vmem),
-        scratch_shapes=[pltpu.VMEM((rows, columns), jnp.float32), pltpu.SemaphoreType.DMA((4,))],
+        scratch_shapes=[pltpu.VMEM((rows, columns), jnp.float32), pltpu.SemaphoreType.DMA((8,))],
         cost_estimate=pl.CostEstimate(
             flops=2 * rows * depth * columns, bytes_accessed=2 * rows * depth, transcendentals=0
         ),

time: 68.9 us -> 68.9 us (level)
  no operation moved by 1% of the time
where the time goes in v8:
time: 68.9 us; the launch traced here: 68.7 us
  blocking collectives  63.1 us (92%)
  Pallas kernels  3.19 us (5%)
  other arithmetic  1.32 us (2%)
  between operations  0.72 us (1%)
    all_gather x1, blocking collectives, on_device(): panel = lax.all_gather(pair, ('y', 'c'), axis=0, tiled=False)  38.1 us
    all_to_all x1, blocking collectives, on_device(): terms = lax.all_to_all(terms, ('xl', 'z'), 0, 0, tiled=True)  18.4 us
    all_gather x1, blocking collectives, on_device(): pair = lax.all_gather(integrals, 'xh', axis=0, tiled=False)  6.64 us
    pallas_call x1, Pallas kernels, on_device(): pl.pallas_call(functools.partial(ladder, (xh, y, c, part)), out_shape=(ja...  3.19 us

profile of v8, /device:TPU:1, one launch (start us, length us, event | category | flops | bytes accessed | tf_op | source)
XLA Modules:
  0.0 68.7 jit_solution(15486581128784315316)
XLA Ops:
  0.6 0.0 copy-start.2
  0.6 6.6 %all-gather = bf16[384,256]{1,0:T(8,128)(2,1)S(1)} all-gather(bf16[192,256]{1,0:T(8,128)(2,1)} %param.8), channel_id=2, replica_groups=mesh['xh'=2,'y'=8,'c'=2,'xl'=2,'z'=12] {'xh'}, dimensions={0}, use_global_device_ids=true | all-gather | bytes 294912 | tf_op jit(solution)/shard_map/all_gather | solution.py:74
  7.3 0.0 copy-start.1
  7.3 0.0 copy-start
  7.3 38.1 %all-gather.3 = f16[32,192,256]{2,1,0:T(8,128)(2,1)S(1)} all-gather(f16[2,192,256]{2,1,0:T(8,128)(2,1)S(1)} %bitcast.3), channel_id=3, replica_groups=mesh['xh'=2,'y'=8,'c'=2,'xl'=2,'z'=12] {'y','c'}, dimensions={0}, use_global_device_ids=true | all-gather | bytes 3342336 | tf_op jit(solution)/shard_map/all_gather | solution.py:76
  45.4 0.3 slice_convert_fusion.near
  45.7 0.0 copy-done.2
  45.7 0.0 copy-done.1
  45.8 0.0 copy-done
  45.8 0.0 copy-start.3
  45.8 0.0 copy-start.4
  45.8 0.3 slice_convert_fusion.1.far
  46.1 0.3 copy-done.3
  46.5 0.0 copy-done.4
  46.5 3.2 %ladder.1 = (f32[512,256]{1,0:T(8,128)}, f32[24,1,512]{2,1,0:T(1,128)S(1)}) custom-call(s32[8,48]{1,0:T(8,128)S(1)} %copy-done.3, s32[2,48]{1,0:T(2,128)S(1)} %bitcast.2, bf16[512,6144]{1,0:T(8,128)(2,1)S(1)} %copy-done, bf16[16,192,256]{2,1,0:T(8,128)(2,1)S(1)} %slice_convert_fusion.near, bf16[16,192,256]{2,1,0:T(8,128)(2,1)S(1)} %slice_convert_fusion.1.far, ...), custom_call_target="tpu_custom_call" | custom-call | flops 1610612736 | bytes 6291456 | tf_op jit(solution)/shard_map/ladder/pallas_call | solution.py:92
  49.7 18.4 %all_to_all.5 = f32[24,1,512]{2,1,0:T(1,128)S(1)} all-to-all(f32[24,1,512]{2,1,0:T(1,128)S(1)} %get-tuple-element.11), channel_id=1, replica_groups=mesh['xh'=2,'y'=8,'c'=2,'xl'=2,'z'=12] {'xl','z'}, dimensions={0} | all-to-all | bytes 98304 | tf_op jit(solution)/shard_map/all_to_all | solution.py:107
  68.0 0.6 reduce_sum.9
  (2 shorter events, 0.1 us)
Async XLA Ops:
  0.6 45.1 %copy-start.2 = (bf16[512,256]{1,0:T(8,128)(2,1)S(1)}, bf16[512,256]{1,0:T(8,128)(2,1)}, u32[]{:S(2)}) copy-start(bf16[512,256]{1,0:T(8,128)(2,1)} %exchange.3) | copy-start | bytes 786436
  7.3 38.5 %copy-start.1 = (f32[512,256]{1,0:T(8,128)S(1)}, f32[512,256]{1,0:T(8,128)}, u32[]{:S(2)}) copy-start(f32[512,256]{1,0:T(8,128)} %residual_in.3) | copy-start | bytes 1572868
  7.3 38.4 %copy-start = (bf16[512,6144]{1,0:T(8,128)(2,1)S(1)}, bf16[512,6144]{1,0:T(8,128)(2,1)}, u32[]{:S(2)}) copy-start(bf16[512,6144]{1,0:T(8,128)(2,1)} %amplitudes.3) | copy-start | bytes 18874372
  45.8 0.7 %copy-start.3 = (s32[8,48]{1,0:T(8,128)S(1)}, s32[8,48]{1,0:T(8,128)}, u32[]{:S(2)}) copy-start(s32[8,48]{1,0:T(8,128)} %amp_map.1) | copy-start | bytes 4612
  45.8 0.7 copy-start.4
